TPU v7x, 128 devices: a whole 4x4x4 slice. The times are simulated.
128 devices in a mesh: shot: 16 (over z, x_hi, core), tile: 8 (over x_lo, y).
Axes of the slice: x: 4 (x_hi: 2, x_lo: 2; x = x_hi * 2 + x_lo), y: 4, z: 4, core: 2. Of those that a mesh axis runs over, the one named last changes fastest.
Arguments:
- lame_lambda: float32 [512, 32, 256], P(('shot', 'tile')), may hold values from 1 to 2
- lame_mu: float32 [512, 32, 256], P(('shot', 'tile')), may hold values from 0.5 to 1
- buoyancy: float32 [512, 32, 256], P(('shot', 'tile')), may hold values from 0.5 to 1
- aperture_row: int32 [16], replicated, may hold values from 0 to 15
- wave_state: float32 [16, 9, 32, 32, 256], P('shot', None, 'tile'), may hold values from -6 to 6
- source_cell: int32 [16], P('shot'), may hold values from 0 to 262143
- wavelet: float32 [16, 12], P('shot'), may hold values from -12 to 12
- receiver_cell: int32 [16, 256], P('shot'), may hold values from 0 to 262143
- prev_row: int32 [16], replicated, may hold values from 0 to 15
- prev_grad: float32 [16, 32, 32, 256], P('shot', 'tile'), may hold values from -6 to 6
Outputs:
- final_state: float32 [16, 9, 32, 32, 256], P('shot', None, 'tile')
- image_sum: float32 [16, 32, 32, 256], P('shot', 'tile')
- owner_grad: float32 [512, 32, 256], P(('shot', 'tile'))
- traces: float32 [16, 12, 256], P('shot')
Inputs may be any that keep to these rules, and one draw needn't show every extreme that they name: `aperture_row`: row q of model tiles holds the cells with x from q * 32 to q * 32 + 31; several shots may share a row and some rows have none. `prev_row`: rows of the previous batch, in the same sense. `source_cell`: flat index x * 32 * 256 + y * 256 + z within the shot's aperture. `receiver_cell`: flat indices as for source_cell; two receivers may share a cell.
All inputs are finite; a program needn't handle non-finite values.
Results may differ from a plain program's by a relative error of at most 0.0003.
Values sent between devices are 32-bit elements; how exact they have to be, the bound alone decides.
A program may use at most 64 MiB of HBM per device.

v0:
```python
import jax
import jax.numpy as jnp
from jax import lax
from jax.sharding import PartitionSpec as P

coefficients = (0.8, -0.2, 4.0 / 105.0, -1.0 / 280.0)
time_step = 0.2


def extended(cells, sides, width):
    for axis, dim in sides:
        count = lax.axis_size(axis)
        ends = count - 1
        head = lax.slice_in_dim(cells, 0, width, axis=dim)
        tail = lax.slice_in_dim(cells, cells.shape[dim] - width, cells.shape[dim], axis=dim)
        cells = jnp.concatenate(
            [
                lax.ppermute(tail, axis, [(i, (i + 1) % count) for i in range(ends)]),
                cells,
                lax.ppermute(head, axis, [((i + 1) % count, i) for i in range(ends)]),
            ],
            axis=dim,
        )
    return cells


def central(padded, axis, length):
    result = None
    for neighbor in range(1, 5):
        forward = lax.slice_in_dim(padded, 4 + neighbor, 4 + neighbor + length, axis=axis)
        backward = lax.slice_in_dim(padded, 4 - neighbor, 4 - neighbor + length, axis=axis)
        term = coefficients[neighbor - 1] * (forward - backward)
        result = term if result is None else result + term
    return result


def derive(field, axis):
    widths = [(0, 0)] * field.ndim
    widths[axis] = (4, 4)
    return central(jnp.pad(field, widths), axis, field.shape[axis])


def inject(velocity_z, buoy_cells, where_local, amplitude):
    flat = velocity_z.reshape(-1)
    count = flat.shape[0]
    inside = (where_local >= 0) & (where_local < count)
    index_at = jnp.clip(where_local, 0, count - 1)
    added = jnp.where(inside, time_step * buoy_cells.reshape(-1)[index_at] * amplitude, 0.0)
    return flat.at[index_at].add(added).reshape(velocity_z.shape)


def sample_at(velocity_z, where_local):
    flat = velocity_z.reshape(-1)
    count = flat.shape[0]
    inside = (where_local >= 0) & (where_local < count)
    index_at = jnp.clip(where_local, 0, count - 1)
    return jnp.where(inside, flat[index_at], 0.0)


def pad_stress(stacked):
    return extended(stacked, (("tile", 1),), 4)


def pad_velocity(stacked):
    return extended(stacked, (("tile", 1),), 4)


def advance_fields(fields, buoy_cells, lambda_cells, shear_cells, source_local, amplitude):
    (
        velocity_x,
        velocity_y,
        velocity_z,
        stress_xx,
        stress_yy,
        stress_zz,
        stress_xy,
        stress_xz,
        stress_yz,
    ) = fields
    length = velocity_x.shape[0]
    stress_dx = central(pad_stress(jnp.stack([stress_xx, stress_xy, stress_xz])), 1, length)
    velocity_x = velocity_x + time_step * buoy_cells * (
        stress_dx[0] + derive(stress_xy, 1) + derive(stress_xz, 2)
    )
    velocity_y = velocity_y + time_step * buoy_cells * (
        stress_dx[1] + derive(stress_yy, 1) + derive(stress_yz, 2)
    )
    velocity_z = velocity_z + time_step * buoy_cells * (
        stress_dx[2] + derive(stress_yz, 1) + derive(stress_zz, 2)
    )
    velocity_z = inject(velocity_z, buoy_cells, source_local, amplitude)
    velocity_dx = central(pad_velocity(jnp.stack([velocity_x, velocity_y, velocity_z])), 1, length)
    strain_xx = velocity_dx[0]
    strain_yy = derive(velocity_y, 1)
    strain_zz = derive(velocity_z, 2)
    dilation = strain_xx + strain_yy + strain_zz
    stress_xx = stress_xx + time_step * (lambda_cells * dilation + 2.0 * shear_cells * strain_xx)
    stress_yy = stress_yy + time_step * (lambda_cells * dilation + 2.0 * shear_cells * strain_yy)
    stress_zz = stress_zz + time_step * (lambda_cells * dilation + 2.0 * shear_cells * strain_zz)
    stress_xy = stress_xy + time_step * shear_cells * (derive(velocity_x, 1) + velocity_dx[1])
    stress_xz = stress_xz + time_step * shear_cells * (derive(velocity_x, 2) + velocity_dx[2])
    stress_yz = stress_yz + time_step * shear_cells * (
        derive(velocity_y, 2) + derive(velocity_z, 1)
    )
    increment = dilation * (stress_xx + stress_yy + stress_zz)
    fields = (
        velocity_x,
        velocity_y,
        velocity_z,
        stress_xx,
        stress_yy,
        stress_zz,
        stress_xy,
        stress_xz,
        stress_yz,
    )
    return (fields, increment)


def on_device(
    lame_lambda,
    lame_mu,
    buoyancy,
    aperture_row,
    wave_state,
    source_cell,
    wavelet,
    receiver_cell,
    prev_row,
    prev_grad,
):
    cells_x = lame_lambda.shape[0]
    shot_index = lax.axis_index("shot")
    tile_index = lax.axis_index("tile")
    my_row = aperture_row[shot_index]
    blank = (jnp.zeros_like(lame_lambda), jnp.zeros_like(lame_mu), jnp.zeros_like(buoyancy))
    pieces = (
        lax.all_gather(lame_lambda, "shot", axis=0, tiled=True),
        lax.all_gather(lame_mu, "shot", axis=0, tiled=True),
        lax.all_gather(buoyancy, "shot", axis=0, tiled=True),
    )
    offset = my_row * cells_x
    span = pieces[0].shape[0]
    inside = (offset >= 0) & (offset < span)
    begin = jnp.clip(offset, 0, span - cells_x)
    lambda_cells, shear_cells, buoy_cells = tuple(
        (
            jnp.where(inside, lax.dynamic_slice_in_dim(piece, begin, cells_x, 0), former)
            for piece, former in zip(pieces, blank)
        )
    )
    local_cells = cells_x * lame_lambda.shape[1] * lame_lambda.shape[2]
    first_cell = tile_index * local_cells
    source_local = source_cell[0] - first_cell
    receivers_local = receiver_cell[0] - first_cell
    state = wave_state[0]
    fields = tuple((state[index] for index in range(9)))

    def advance(carried, amplitude):
        fields, image_sum = carried
        fields, increment = advance_fields(
            fields, buoy_cells, lambda_cells, shear_cells, source_local, amplitude
        )
        record = sample_at(fields[2], receivers_local)
        record = lax.psum(record, "tile")
        return ((fields, image_sum + increment), record)

    (fields, image_sum), records = lax.scan(advance, (fields, jnp.zeros_like(state[0])), wavelet[0])
    grad_local = prev_grad[0]
    target = prev_row[shot_index]
    copies = cells_x * lax.axis_size("shot") // cells_x
    slot = jnp.arange(cells_x * lax.axis_size("shot"), dtype=jnp.int32) // cells_x
    owner_grad = lax.psum_scatter(
        jnp.where((slot == target)[:, None, None], jnp.tile(grad_local, (copies, 1, 1)), 0.0),
        "shot",
        scatter_dimension=0,
        tiled=True,
    )
    return (jnp.stack(fields)[None], image_sum[None], owner_grad, records[None])


def solution(mesh):
    placed = (
        P(("shot", "tile"), None, None),
        P(("shot", "tile"), None, None),
        P(("shot", "tile"), None, None),
        P(),
        P("shot", None, "tile", None, None),
        P("shot"),
        P("shot", None),
        P("shot", None),
        P(),
        P("shot", "tile", None, None),
    )
    return jax.shard_map(
        on_device,
        mesh=mesh,
        in_specs=placed,
        out_specs=(
            P("shot", None, "tile", None, None),
            P("shot", "tile", None, None),
            P(("shot", "tile"), None, None),
            P("shot", None, None),
        ),
        check_vma=False,
    )
```

profile of v0, /device:TPU:2, one launch (start us, length us, event | category | flops | bytes accessed | tf_op | source)
XLA Modules:
  0.0 700.0 jit_solution(10449325736466602303)
XLA Ops:
  17.0 42.5 %all-gather.4.cloned.1.call-done = f32[64,32,256]{2,1,0:T(8,128)} async-done(((f32[4,32,256]{2,1,0:T(8,128)}), f32[64,32,256]{2,1,0:T(8,128)}) %all-gather.4.cloned.1.call-update) | async-done | bytes 2097168 | tf_op jit(solution)/shard_map/all_gather | solution.py:140
  61.9 46.6 %all-gather.8.cloned.1.call-done = f32[64,32,256]{2,1,0:T(8,128)} async-done(((f32[4,32,256]{2,1,0:T(8,128)}), f32[64,32,256]{2,1,0:T(8,128)}) %all-gather.8.cloned.1.call-update) | async-done | bytes 2097168 | tf_op jit(solution)/shard_map/all_gather | solution.py:139
  109.4 48.0 %all-gather.6.cloned.1.call-done = f32[64,32,256]{2,1,0:T(8,128)} async-done(((f32[4,32,256]{2,1,0:T(8,128)}), f32[64,32,256]{2,1,0:T(8,128)}) %all-gather.6.cloned.1.call-update) | async-done | bytes 2097168 | tf_op jit(solution)/shard_map/all_gather | solution.py:138
  158.4 533.3 %while.34 = (s32[]{:T(128)}, f32[4,32,256]{2,1,0:T(8,128)S(1)}, f32[4,32,256]{2,1,0:T(8,128)S(1)}, f32[4,32,256]{2,1,0:T(8,128)S(1)}, f32[4,32,256]{2,1,0:T(8,12...) while((s32[]{:T(128)}, f32[4,32,256]{2,1,0:T(8,128)S(1)}, ...), condition=%wide.region_2.3_spmd.clone, body=%wide.region_0.2_spmd.clone.sunk | while | flops 10718471 | bytes 27152824 | solution.py:168
  158.4 5.5 collective-permute-start
  167.1 5.6 collective-permute-done
  172.7 6.2 collective-permute-done.1
  188.2 18.3 %psum.12 = f32[1,256]{1,0:T(1,128)S(1)} all-reduce(f32[1,256]{1,0:T(1,128)S(1)} %bitcast.139), channel_id=1, replica_groups=mesh['shot'=16,'tile'=8] {'tile'}, use_global_device_ids=true, to_apply=%region_1.1 | all-reduce | flops 256 | bytes 2048 | tf_op jit(solution)/shard_map/while/body/eval_jaxpr/psum | solution.py:165
  217.6 6.8 collective-permute-done.1
  233.8 18.1 %psum.12 = f32[1,256]{1,0:T(1,128)S(1)} all-reduce(f32[1,256]{1,0:T(1,128)S(1)} %bitcast.139), channel_id=1, replica_groups=mesh['shot'=16,'tile'=8] {'tile'}, use_global_device_ids=true, to_apply=%region_1.1 | all-reduce | flops 256 | bytes 2048 | tf_op jit(solution)/shard_map/while/body/eval_jaxpr/psum | solution.py:165
  277.3 18.1 %psum.12 = f32[1,256]{1,0:T(1,128)S(1)} all-reduce(f32[1,256]{1,0:T(1,128)S(1)} %bitcast.139), channel_id=1, replica_groups=mesh['shot'=16,'tile'=8] {'tile'}, use_global_device_ids=true, to_apply=%region_1.1 | all-reduce | flops 256 | bytes 2048 | tf_op jit(solution)/shard_map/while/body/eval_jaxpr/psum | solution.py:165
  304.0 4.6 collective-permute-done
  322.0 18.2 %psum.12 = f32[1,256]{1,0:T(1,128)S(1)} all-reduce(f32[1,256]{1,0:T(1,128)S(1)} %bitcast.139), channel_id=1, replica_groups=mesh['shot'=16,'tile'=8] {'tile'}, use_global_device_ids=true, to_apply=%region_1.1 | all-reduce | flops 256 | bytes 2048 | tf_op jit(solution)/shard_map/while/body/eval_jaxpr/psum | solution.py:165
  364.7 19.1 %psum.12 = f32[1,256]{1,0:T(1,128)S(1)} all-reduce(f32[1,256]{1,0:T(1,128)S(1)} %bitcast.139), channel_id=1, replica_groups=mesh['shot'=16,'tile'=8] {'tile'}, use_global_device_ids=true, to_apply=%region_1.1 | all-reduce | flops 256 | bytes 2048 | tf_op jit(solution)/shard_map/while/body/eval_jaxpr/psum | solution.py:165
  394.9 6.0 collective-permute-done.1
  410.2 18.2 %psum.12 = f32[1,256]{1,0:T(1,128)S(1)} all-reduce(f32[1,256]{1,0:T(1,128)S(1)} %bitcast.139), channel_id=1, replica_groups=mesh['shot'=16,'tile'=8] {'tile'}, use_global_device_ids=true, to_apply=%region_1.1 | all-reduce | flops 256 | bytes 2048 | tf_op jit(solution)/shard_map/while/body/eval_jaxpr/psum | solution.py:165
  452.8 18.2 %psum.12 = f32[1,256]{1,0:T(1,128)S(1)} all-reduce(f32[1,256]{1,0:T(1,128)S(1)} %bitcast.139), channel_id=1, replica_groups=mesh['shot'=16,'tile'=8] {'tile'}, use_global_device_ids=true, to_apply=%region_1.1 | all-reduce | flops 256 | bytes 2048 | tf_op jit(solution)/shard_map/while/body/eval_jaxpr/psum | solution.py:165
  496.9 18.1 %psum.12 = f32[1,256]{1,0:T(1,128)S(1)} all-reduce(f32[1,256]{1,0:T(1,128)S(1)} %bitcast.139), channel_id=1, replica_groups=mesh['shot'=16,'tile'=8] {'tile'}, use_global_device_ids=true, to_apply=%region_1.1 | all-reduce | flops 256 | bytes 2048 | tf_op jit(solution)/shard_map/while/body/eval_jaxpr/psum | solution.py:165
  523.5 4.5 collective-permute-done
  528.0 5.8 collective-permute-done.1
  543.1 18.1 %psum.12 = f32[1,256]{1,0:T(1,128)S(1)} all-reduce(f32[1,256]{1,0:T(1,128)S(1)} %bitcast.139), channel_id=1, replica_groups=mesh['shot'=16,'tile'=8] {'tile'}, use_global_device_ids=true, to_apply=%region_1.1 | all-reduce | flops 256 | bytes 2048 | tf_op jit(solution)/shard_map/while/body/eval_jaxpr/psum | solution.py:165
  586.0 18.1 %psum.12 = f32[1,256]{1,0:T(1,128)S(1)} all-reduce(f32[1,256]{1,0:T(1,128)S(1)} %bitcast.139), channel_id=1, replica_groups=mesh['shot'=16,'tile'=8] {'tile'}, use_global_device_ids=true, to_apply=%region_1.1 | all-reduce | flops 256 | bytes 2048 | tf_op jit(solution)/shard_map/while/body/eval_jaxpr/psum | solution.py:165
  629.5 18.1 %psum.12 = f32[1,256]{1,0:T(1,128)S(1)} all-reduce(f32[1,256]{1,0:T(1,128)S(1)} %bitcast.139), channel_id=1, replica_groups=mesh['shot'=16,'tile'=8] {'tile'}, use_global_device_ids=true, to_apply=%region_1.1 | all-reduce | flops 256 | bytes 2048 | tf_op jit(solution)/shard_map/while/body/eval_jaxpr/psum | solution.py:165
  672.1 18.1 %psum.12 = f32[1,256]{1,0:T(1,128)S(1)} all-reduce(f32[1,256]{1,0:T(1,128)S(1)} %bitcast.139), channel_id=1, replica_groups=mesh['shot'=16,'tile'=8] {'tile'}, use_global_device_ids=true, to_apply=%region_1.1 | all-reduce | flops 256 | bytes 2048 | tf_op jit(solution)/shard_map/while/body/eval_jaxpr/psum | solution.py:165
  (372 shorter events, 273.6 us)
Async XLA Ops:
  7.2 52.4 %all-gather.4.cloned.1.call-start = ((), (), s32[]{:S(2)}) async-start(), calls=%async_computation.1 | async-start | bytes 2228224 | tf_op jit(solution)/shard_map/all_gather | solution.py:140
  7.9 100.6 %all-gather.8.cloned.1.call-start = ((), (), s32[]{:S(2)}) async-start(), calls=%async_computation.3 | async-start | bytes 2228224 | tf_op jit(solution)/shard_map/all_gather | solution.py:139
  8.6 148.8 %all-gather.6.cloned.1.call-start = ((), (), s32[]{:S(2)}) async-start(), calls=%async_computation.2 | async-start | bytes 2228224 | tf_op jit(solution)/shard_map/all_gather | solution.py:138
  9.4 683.1 %reduce-scatter.2.cloned.1.call-start = ((), (), s32[]{:S(2)}) async-start(), calls=%async_computation.4 | async-start | bytes 2228224 | tf_op jit(solution)/shard_map/reduce_scatter | solution.py:173
  180.6 26.0 %collective-permute-start.2 = (f32[3,4,32,256]{3,2,1,0:T(8,128)S(1)}, f32[3,4,32,256]{3,2,1,0:T(8,128)S(1)}, u32[]{:S(2)}, u32[]{:S(2)}) collective-permute-start(f32[3,4,32,256]{3,2,1,0:T(8,128)S(1)} %pad_maximum_fusion.10), channel_id=1, source_target_pairs={{1,0},{2,1},{3,2},{4,3},{5,4},{6,5},{7,6},{9,8},{10,9},{11,10},{12... | collective-permute-start | bytes 1179656 | tf_op jit(solution)/shard_map/while/body/eval_jaxpr/ppermute | solution.py:20
  182.5 24.1 %collective-permute-start.3 = (f32[3,4,32,256]{3,2,1,0:T(8,128)S(1)}, f32[3,4,32,256]{3,2,1,0:T(8,128)S(1)}, u32[]{:S(2)}, u32[]{:S(2)}) collective-permute-start(f32[3,4,32,256]{3,2,1,0:T(8,128)S(1)} %pad_maximum_fusion.10), channel_id=1, source_target_pairs={{0,1},{1,2},{2,3},{3,4},{4,5},{5,6},{6,7},{8,9},{9,10},{10,11},{11... | collective-permute-start | bytes 1179656 | tf_op jit(solution)/shard_map/while/body/eval_jaxpr/ppermute | solution.py:18
  226.1 25.8 %collective-permute-start.2 = (f32[3,4,32,256]{3,2,1,0:T(8,128)S(1)}, f32[3,4,32,256]{3,2,1,0:T(8,128)S(1)}, u32[]{:S(2)}, u32[]{:S(2)}) collective-permute-start(f32[3,4,32,256]{3,2,1,0:T(8,128)S(1)} %pad_maximum_fusion.10), channel_id=1, source_target_pairs={{1,0},{2,1},{3,2},{4,3},{5,4},{6,5},{7,6},{9,8},{10,9},{11,10},{12... | collective-permute-start | bytes 1179656 | tf_op jit(solution)/shard_map/while/body/eval_jaxpr/ppermute | solution.py:20
  228.0 23.9 %collective-permute-start.3 = (f32[3,4,32,256]{3,2,1,0:T(8,128)S(1)}, f32[3,4,32,256]{3,2,1,0:T(8,128)S(1)}, u32[]{:S(2)}, u32[]{:S(2)}) collective-permute-start(f32[3,4,32,256]{3,2,1,0:T(8,128)S(1)} %pad_maximum_fusion.10), channel_id=1, source_target_pairs={{0,1},{1,2},{2,3},{3,4},{4,5},{5,6},{6,7},{8,9},{9,10},{10,11},{11... | collective-permute-start | bytes 1179656 | tf_op jit(solution)/shard_map/while/body/eval_jaxpr/ppermute | solution.py:18
  269.6 25.8 %collective-permute-start.2 = (f32[3,4,32,256]{3,2,1,0:T(8,128)S(1)}, f32[3,4,32,256]{3,2,1,0:T(8,128)S(1)}, u32[]{:S(2)}, u32[]{:S(2)}) collective-permute-start(f32[3,4,32,256]{3,2,1,0:T(8,128)S(1)} %pad_maximum_fusion.10), channel_id=1, source_target_pairs={{1,0},{2,1},{3,2},{4,3},{5,4},{6,5},{7,6},{9,8},{10,9},{11,10},{12... | collective-permute-start | bytes 1179656 | tf_op jit(solution)/shard_map/while/body/eval_jaxpr/ppermute | solution.py:20
  271.6 23.9 %collective-permute-start.3 = (f32[3,4,32,256]{3,2,1,0:T(8,128)S(1)}, f32[3,4,32,256]{3,2,1,0:T(8,128)S(1)}, u32[]{:S(2)}, u32[]{:S(2)}) collective-permute-start(f32[3,4,32,256]{3,2,1,0:T(8,128)S(1)} %pad_maximum_fusion.10), channel_id=1, source_target_pairs={{0,1},{1,2},{2,3},{3,4},{4,5},{5,6},{6,7},{8,9},{9,10},{10,11},{11... | collective-permute-start | bytes 1179656 | tf_op jit(solution)/shard_map/while/body/eval_jaxpr/ppermute | solution.py:18
  314.3 25.9 %collective-permute-start.2 = (f32[3,4,32,256]{3,2,1,0:T(8,128)S(1)}, f32[3,4,32,256]{3,2,1,0:T(8,128)S(1)}, u32[]{:S(2)}, u32[]{:S(2)}) collective-permute-start(f32[3,4,32,256]{3,2,1,0:T(8,128)S(1)} %pad_maximum_fusion.10), channel_id=1, source_target_pairs={{1,0},{2,1},{3,2},{4,3},{5,4},{6,5},{7,6},{9,8},{10,9},{11,10},{12... | collective-permute-start | bytes 1179656 | tf_op jit(solution)/shard_map/while/body/eval_jaxpr/ppermute | solution.py:20
  316.2 23.9 %collective-permute-start.3 = (f32[3,4,32,256]{3,2,1,0:T(8,128)S(1)}, f32[3,4,32,256]{3,2,1,0:T(8,128)S(1)}, u32[]{:S(2)}, u32[]{:S(2)}) collective-permute-start(f32[3,4,32,256]{3,2,1,0:T(8,128)S(1)} %pad_maximum_fusion.10), channel_id=1, source_target_pairs={{0,1},{1,2},{2,3},{3,4},{4,5},{5,6},{6,7},{8,9},{9,10},{10,11},{11... | collective-permute-start | bytes 1179656 | tf_op jit(solution)/shard_map/while/body/eval_jaxpr/ppermute | solution.py:18
  357.0 26.8 %collective-permute-start.2 = (f32[3,4,32,256]{3,2,1,0:T(8,128)S(1)}, f32[3,4,32,256]{3,2,1,0:T(8,128)S(1)}, u32[]{:S(2)}, u32[]{:S(2)}) collective-permute-start(f32[3,4,32,256]{3,2,1,0:T(8,128)S(1)} %pad_maximum_fusion.10), channel_id=1, source_target_pairs={{1,0},{2,1},{3,2},{4,3},{5,4},{6,5},{7,6},{9,8},{10,9},{11,10},{12... | collective-permute-start | bytes 1179656 | tf_op jit(solution)/shard_map/while/body/eval_jaxpr/ppermute | solution.py:20
  358.9 24.9 %collective-permute-start.3 = (f32[3,4,32,256]{3,2,1,0:T(8,128)S(1)}, f32[3,4,32,256]{3,2,1,0:T(8,128)S(1)}, u32[]{:S(2)}, u32[]{:S(2)}) collective-permute-start(f32[3,4,32,256]{3,2,1,0:T(8,128)S(1)} %pad_maximum_fusion.10), channel_id=1, source_target_pairs={{0,1},{1,2},{2,3},{3,4},{4,5},{5,6},{6,7},{8,9},{9,10},{10,11},{11... | collective-permute-start | bytes 1179656 | tf_op jit(solution)/shard_map/while/body/eval_jaxpr/ppermute | solution.py:18
  402.5 25.9 %collective-permute-start.2 = (f32[3,4,32,256]{3,2,1,0:T(8,128)S(1)}, f32[3,4,32,256]{3,2,1,0:T(8,128)S(1)}, u32[]{:S(2)}, u32[]{:S(2)}) collective-permute-start(f32[3,4,32,256]{3,2,1,0:T(8,128)S(1)} %pad_maximum_fusion.10), channel_id=1, source_target_pairs={{1,0},{2,1},{3,2},{4,3},{5,4},{6,5},{7,6},{9,8},{10,9},{11,10},{12... | collective-permute-start | bytes 1179656 | tf_op jit(solution)/shard_map/while/body/eval_jaxpr/ppermute | solution.py:20
  404.4 23.9 %collective-permute-start.3 = (f32[3,4,32,256]{3,2,1,0:T(8,128)S(1)}, f32[3,4,32,256]{3,2,1,0:T(8,128)S(1)}, u32[]{:S(2)}, u32[]{:S(2)}) collective-permute-start(f32[3,4,32,256]{3,2,1,0:T(8,128)S(1)} %pad_maximum_fusion.10), channel_id=1, source_target_pairs={{0,1},{1,2},{2,3},{3,4},{4,5},{5,6},{6,7},{8,9},{9,10},{10,11},{11... | collective-permute-start | bytes 1179656 | tf_op jit(solution)/shard_map/while/body/eval_jaxpr/ppermute | solution.py:18
  445.2 25.9 %collective-permute-start.2 = (f32[3,4,32,256]{3,2,1,0:T(8,128)S(1)}, f32[3,4,32,256]{3,2,1,0:T(8,128)S(1)}, u32[]{:S(2)}, u32[]{:S(2)}) collective-permute-start(f32[3,4,32,256]{3,2,1,0:T(8,128)S(1)} %pad_maximum_fusion.10), channel_id=1, source_target_pairs={{1,0},{2,1},{3,2},{4,3},{5,4},{6,5},{7,6},{9,8},{10,9},{11,10},{12... | collective-permute-start | bytes 1179656 | tf_op jit(solution)/shard_map/while/body/eval_jaxpr/ppermute | solution.py:20
  447.1 23.9 %collective-permute-start.3 = (f32[3,4,32,256]{3,2,1,0:T(8,128)S(1)}, f32[3,4,32,256]{3,2,1,0:T(8,128)S(1)}, u32[]{:S(2)}, u32[]{:S(2)}) collective-permute-start(f32[3,4,32,256]{3,2,1,0:T(8,128)S(1)} %pad_maximum_fusion.10), channel_id=1, source_target_pairs={{0,1},{1,2},{2,3},{3,4},{4,5},{5,6},{6,7},{8,9},{9,10},{10,11},{11... | collective-permute-start | bytes 1179656 | tf_op jit(solution)/shard_map/while/body/eval_jaxpr/ppermute | solution.py:18
  489.2 25.8 %collective-permute-start.2 = (f32[3,4,32,256]{3,2,1,0:T(8,128)S(1)}, f32[3,4,32,256]{3,2,1,0:T(8,128)S(1)}, u32[]{:S(2)}, u32[]{:S(2)}) collective-permute-start(f32[3,4,32,256]{3,2,1,0:T(8,128)S(1)} %pad_maximum_fusion.10), channel_id=1, source_target_pairs={{1,0},{2,1},{3,2},{4,3},{5,4},{6,5},{7,6},{9,8},{10,9},{11,10},{12... | collective-permute-start | bytes 1179656 | tf_op jit(solution)/shard_map/while/body/eval_jaxpr/ppermute | solution.py:20
  535.4 25.8 %collective-permute-start.2 = (f32[3,4,32,256]{3,2,1,0:T(8,128)S(1)}, f32[3,4,32,256]{3,2,1,0:T(8,128)S(1)}, u32[]{:S(2)}, u32[]{:S(2)}) collective-permute-start(f32[3,4,32,256]{3,2,1,0:T(8,128)S(1)} %pad_maximum_fusion.10), channel_id=1, source_target_pairs={{1,0},{2,1},{3,2},{4,3},{5,4},{6,5},{7,6},{9,8},{10,9},{11,10},{12... | collective-permute-start | bytes 1179656 | tf_op jit(solution)/shard_map/while/body/eval_jaxpr/ppermute | solution.py:20
  578.3 25.8 %collective-permute-start.2 = (f32[3,4,32,256]{3,2,1,0:T(8,128)S(1)}, f32[3,4,32,256]{3,2,1,0:T(8,128)S(1)}, u32[]{:S(2)}, u32[]{:S(2)}) collective-permute-start(f32[3,4,32,256]{3,2,1,0:T(8,128)S(1)} %pad_maximum_fusion.10), channel_id=1, source_target_pairs={{1,0},{2,1},{3,2},{4,3},{5,4},{6,5},{7,6},{9,8},{10,9},{11,10},{12... | collective-permute-start | bytes 1179656 | tf_op jit(solution)/shard_map/while/body/eval_jaxpr/ppermute | solution.py:20
  580.2 23.9 %collective-permute-start.3 = (f32[3,4,32,256]{3,2,1,0:T(8,128)S(1)}, f32[3,4,32,256]{3,2,1,0:T(8,128)S(1)}, u32[]{:S(2)}, u32[]{:S(2)}) collective-permute-start(f32[3,4,32,256]{3,2,1,0:T(8,128)S(1)} %pad_maximum_fusion.10), channel_id=1, source_target_pairs={{0,1},{1,2},{2,3},{3,4},{4,5},{5,6},{6,7},{8,9},{9,10},{10,11},{11... | collective-permute-start | bytes 1179656 | tf_op jit(solution)/shard_map/while/body/eval_jaxpr/ppermute | solution.py:18
  621.9 25.8 %collective-permute-start.2 = (f32[3,4,32,256]{3,2,1,0:T(8,128)S(1)}, f32[3,4,32,256]{3,2,1,0:T(8,128)S(1)}, u32[]{:S(2)}, u32[]{:S(2)}) collective-permute-start(f32[3,4,32,256]{3,2,1,0:T(8,128)S(1)} %pad_maximum_fusion.10), channel_id=1, source_target_pairs={{1,0},{2,1},{3,2},{4,3},{5,4},{6,5},{7,6},{9,8},{10,9},{11,10},{12... | collective-permute-start | bytes 1179656 | tf_op jit(solution)/shard_map/while/body/eval_jaxpr/ppermute | solution.py:20
  664.4 25.8 %collective-permute-start.2 = (f32[3,4,32,256]{3,2,1,0:T(8,128)S(1)}, f32[3,4,32,256]{3,2,1,0:T(8,128)S(1)}, u32[]{:S(2)}, u32[]{:S(2)}) collective-permute-start(f32[3,4,32,256]{3,2,1,0:T(8,128)S(1)} %pad_maximum_fusion.10), channel_id=1, source_target_pairs={{1,0},{2,1},{3,2},{4,3},{5,4},{6,5},{7,6},{9,8},{10,9},{11,10},{12... | collective-permute-start | bytes 1179656 | tf_op jit(solution)/shard_map/while/body/eval_jaxpr/ppermute | solution.py:20
  (34 other events, 525.0 us)
Sparse Core Ops, SparseCore 0:
  10.4 49.0 all-gather.3
  62.0 46.4 all-gather.7
  111.0 46.4 all-gather.5
  161.7 70.1 reduce-scatter.1
where the time goes:
time: 702 us; the launch traced here: 700 us
  waiting for transfers between devices  238 us (34%)
  blocking collectives  218 us (31%)
  starting transfers between devices  142 us (20%)
  other arithmetic  40.5 us (6%)
  local copies, waits for them, and re-layouts  35.4 us (5%)
  between operations  16 us (2%)
  loops' own time  10 us (1%)
    psum x12, blocking collectives, advance(): record = lax.psum(record, 'tile')  218 us
    ppermute x24, starting transfers between devices, extended(): lax.ppermute(tail, axis, [(i, (i + 1) % count) for i in range(ends)])  87 us
    ppermute x24, waiting for transfers between devices, extended(): lax.ppermute(tail, axis, [(i, (i + 1) % count) for i in range(ends)])  57.5 us
    ppermute x24, starting transfers between devices, extended(): lax.ppermute(head, axis, [((i + 1) % count, i) for i in range(ends)])  54.9 us
    all_gather x1, waiting for transfers between devices, on_device(): lax.all_gather(lame_lambda, 'shot', axis=0, tiled=True)  48 us
    all_gather x1, waiting for transfers between devices, on_device(): lax.all_gather(lame_mu, 'shot', axis=0, tiled=True)  46.6 us
    all_gather x1, waiting for transfers between devices, on_device(): lax.all_gather(buoyancy, 'shot', axis=0, tiled=True)  42.5 us
    ppermute x24, waiting for transfers between devices, extended(): lax.ppermute(head, axis, [((i + 1) % count, i) for i in range(ends)])  41.1 us
  transfers between devices with their start and end apart: 52, of which 27 were waited for; matrix products, arithmetic and copies ran while one was open for 11% of the time, Pallas kernels for 0%

commit v1 on v0

--- a/solution.py
+++ b/solution.py
@@ -162,7 +162,7 @@
             fields, buoy_cells, lambda_cells, shear_cells, source_local, amplitude
         )
         record = sample_at(fields[2], receivers_local)
-        record = lax.psum(record, "tile")
+        record = jnp.sum(lax.all_gather(record, "tile"), axis=0)
         return ((fields, image_sum + increment), record)
 
     (fields, image_sum), records = lax.scan(advance, (fields, jnp.zeros_like(state[0])), wavelet[0])

time: 702 us -> 697 us (level)
  blocking collectives: 218 us -> 210 us
    psum x12 -> x0, blocking collectives: 218 us -> none  [advance(): record = lax.psum(record, 'tile')]
    all_gather x0 -> x12, blocking collectives: none -> 210 us  [advance(): record = jnp.sum(lax.all_gather(record, 'tile'), axis=0)]
where the time goes in v1:
time: 697 us; the launch traced here: 696 us
  waiting for transfers between devices  241 us (35%)
  blocking collectives  210 us (30%)
  starting transfers between devices  142 us (20%)
  other arithmetic  40.8 us (6%)
  local copies, waits for them, and re-layouts  35.5 us (5%)
  between operations  16 us (2%)
  loops' own time  10.1 us (1%)
    all_gather x12, blocking collectives, advance(): record = jnp.sum(lax.all_gather(record, 'tile'), axis=0)  210 us
    ppermute x24, starting transfers between devices, extended(): lax.ppermute(tail, axis, [(i, (i + 1) % count) for i in range(ends)])  86.2 us
    ppermute x24, waiting for transfers between devices, extended(): lax.ppermute(tail, axis, [(i, (i + 1) % count) for i in range(ends)])  57.5 us
    ppermute x24, starting transfers between devices, extended(): lax.ppermute(head, axis, [((i + 1) % count, i) for i in range(ends)])  56 us
    all_gather x1, waiting for transfers between devices, on_device(): lax.all_gather(lame_lambda, 'shot', axis=0, tiled=True)  48 us
    all_gather x1, waiting for transfers between devices, on_device(): lax.all_gather(lame_mu, 'shot', axis=0, tiled=True)  46.6 us
    ppermute x24, waiting for transfers between devices, extended(): lax.ppermute(head, axis, [((i + 1) % count, i) for i in range(ends)])  44 us
    all_gather x1, waiting for transfers between devices, on_device(): lax.all_gather(buoyancy, 'shot', axis=0, tiled=True)  42.5 us
  transfers between devices with their start and end apart: 52, of which 27 were waited for; matrix products, arithmetic and copies ran while one was open for 11% of the time, Pallas kernels for 0%

profile of v1, /device:TPU:2, one launch (start us, length us, event | category | flops | bytes accessed | tf_op | source)
XLA Modules:
  0.0 695.5 jit_solution(10302262534648870560)
XLA Ops:
  17.0 42.5 %all-gather.9.cloned.1.call-done = f32[64,32,256]{2,1,0:T(8,128)} async-done(((f32[4,32,256]{2,1,0:T(8,128)}), f32[64,32,256]{2,1,0:T(8,128)}) %all-gather.9.cloned.1.call-update) | async-done | bytes 2097168 | tf_op jit(solution)/shard_map/all_gather | solution.py:140
  61.9 46.6 %all-gather.13.cloned.1.call-done = f32[64,32,256]{2,1,0:T(8,128)} async-done(((f32[4,32,256]{2,1,0:T(8,128)}), f32[64,32,256]{2,1,0:T(8,128)}) %all-gather.13.cloned.1.call-update) | async-done | bytes 2097168 | tf_op jit(solution)/shard_map/all_gather | solution.py:139
  109.4 48.0 %all-gather.11.cloned.1.call-done = f32[64,32,256]{2,1,0:T(8,128)} async-done(((f32[4,32,256]{2,1,0:T(8,128)}), f32[64,32,256]{2,1,0:T(8,128)}) %all-gather.11.cloned.1.call-update) | async-done | bytes 2097168 | tf_op jit(solution)/shard_map/all_gather | solution.py:138
  158.4 528.8 %while.34 = (s32[]{:T(128)}, f32[4,32,256]{2,1,0:T(8,128)S(1)}, f32[4,32,256]{2,1,0:T(8,128)S(1)}, f32[4,32,256]{2,1,0:T(8,128)S(1)}, f32[4,32,256]{2,1,0:T(8,12...) while((s32[]{:T(128)}, f32[4,32,256]{2,1,0:T(8,128)S(1)}, ...), condition=%wide.region_2.3_spmd.clone, body=%wide.region_0.2_spmd.clone.sunk | while | flops 10720007 | bytes 27169212 | solution.py:168
  158.4 5.5 collective-permute-start
  167.1 5.6 collective-permute-done
  172.7 6.2 collective-permute-done.1
  188.2 17.3 %all-gather.4 = f32[8,1,256]{2,1,0:T(1,128)S(1)} all-gather(f32[1,1,256]{2,1,0:T(1,128)S(1)} %bitcast.142), channel_id=2, replica_groups=mesh['shot'=16,'tile'=8] {'tile'}, dimensions={0}, use_global_device_ids=true | all-gather | bytes 9216 | tf_op jit(solution)/shard_map/while/body/eval_jaxpr/all_gather | solution.py:165
  216.8 7.4 %collective-permute-done.1 = f32[3,4,32,256]{3,2,1,0:T(8,128)S(1)} collective-permute-done((f32[3,4,32,256]{3,2,1,0:T(8,128)S(1)}, f32[3,4,32,256]{3,2,1,0:T(8,128)S(1)}, u32[]{:S(2)}, u32[]{:S(2)}) %collective-permute-start.1) | collective-permute-done | bytes 393248 | tf_op jit(solution)/shard_map/while/body/eval_jaxpr/ppermute | solution.py:18
  233.5 17.2 %all-gather.4 = f32[8,1,256]{2,1,0:T(1,128)S(1)} all-gather(f32[1,1,256]{2,1,0:T(1,128)S(1)} %bitcast.142), channel_id=2, replica_groups=mesh['shot'=16,'tile'=8] {'tile'}, dimensions={0}, use_global_device_ids=true | all-gather | bytes 9216 | tf_op jit(solution)/shard_map/while/body/eval_jaxpr/all_gather | solution.py:165
  276.7 17.2 %all-gather.4 = f32[8,1,256]{2,1,0:T(1,128)S(1)} all-gather(f32[1,1,256]{2,1,0:T(1,128)S(1)} %bitcast.142), channel_id=2, replica_groups=mesh['shot'=16,'tile'=8] {'tile'}, dimensions={0}, use_global_device_ids=true | all-gather | bytes 9216 | tf_op jit(solution)/shard_map/while/body/eval_jaxpr/all_gather | solution.py:165
  320.6 17.2 %all-gather.4 = f32[8,1,256]{2,1,0:T(1,128)S(1)} all-gather(f32[1,1,256]{2,1,0:T(1,128)S(1)} %bitcast.142), channel_id=2, replica_groups=mesh['shot'=16,'tile'=8] {'tile'}, dimensions={0}, use_global_device_ids=true | all-gather | bytes 9216 | tf_op jit(solution)/shard_map/while/body/eval_jaxpr/all_gather | solution.py:165
  362.4 18.8 %all-gather.4 = f32[8,1,256]{2,1,0:T(1,128)S(1)} all-gather(f32[1,1,256]{2,1,0:T(1,128)S(1)} %bitcast.142), channel_id=2, replica_groups=mesh['shot'=16,'tile'=8] {'tile'}, dimensions={0}, use_global_device_ids=true | all-gather | bytes 9216 | tf_op jit(solution)/shard_map/while/body/eval_jaxpr/all_gather | solution.py:165
  392.6 6.0 collective-permute-done.1
  407.9 17.2 %all-gather.4 = f32[8,1,256]{2,1,0:T(1,128)S(1)} all-gather(f32[1,1,256]{2,1,0:T(1,128)S(1)} %bitcast.142), channel_id=2, replica_groups=mesh['shot'=16,'tile'=8] {'tile'}, dimensions={0}, use_global_device_ids=true | all-gather | bytes 9216 | tf_op jit(solution)/shard_map/while/body/eval_jaxpr/all_gather | solution.py:165
  449.7 17.2 %all-gather.4 = f32[8,1,256]{2,1,0:T(1,128)S(1)} all-gather(f32[1,1,256]{2,1,0:T(1,128)S(1)} %bitcast.142), channel_id=2, replica_groups=mesh['shot'=16,'tile'=8] {'tile'}, dimensions={0}, use_global_device_ids=true | all-gather | bytes 9216 | tf_op jit(solution)/shard_map/while/body/eval_jaxpr/all_gather | solution.py:165
  475.6 5.4 collective-permute-done
  494.3 18.9 %all-gather.4 = f32[8,1,256]{2,1,0:T(1,128)S(1)} all-gather(f32[1,1,256]{2,1,0:T(1,128)S(1)} %bitcast.142), channel_id=2, replica_groups=mesh['shot'=16,'tile'=8] {'tile'}, dimensions={0}, use_global_device_ids=true | all-gather | bytes 9216 | tf_op jit(solution)/shard_map/while/body/eval_jaxpr/all_gather | solution.py:165
  525.4 5.5 collective-permute-done.1
  540.2 17.2 %all-gather.4 = f32[8,1,256]{2,1,0:T(1,128)S(1)} all-gather(f32[1,1,256]{2,1,0:T(1,128)S(1)} %bitcast.142), channel_id=2, replica_groups=mesh['shot'=16,'tile'=8] {'tile'}, dimensions={0}, use_global_device_ids=true | all-gather | bytes 9216 | tf_op jit(solution)/shard_map/while/body/eval_jaxpr/all_gather | solution.py:165
  581.9 17.2 %all-gather.4 = f32[8,1,256]{2,1,0:T(1,128)S(1)} all-gather(f32[1,1,256]{2,1,0:T(1,128)S(1)} %bitcast.142), channel_id=2, replica_groups=mesh['shot'=16,'tile'=8] {'tile'}, dimensions={0}, use_global_device_ids=true | all-gather | bytes 9216 | tf_op jit(solution)/shard_map/while/body/eval_jaxpr/all_gather | solution.py:165
  607.8 5.6 collective-permute-done
  626.7 17.2 %all-gather.4 = f32[8,1,256]{2,1,0:T(1,128)S(1)} all-gather(f32[1,1,256]{2,1,0:T(1,128)S(1)} %bitcast.142), channel_id=2, replica_groups=mesh['shot'=16,'tile'=8] {'tile'}, dimensions={0}, use_global_device_ids=true | all-gather | bytes 9216 | tf_op jit(solution)/shard_map/while/body/eval_jaxpr/all_gather | solution.py:165
  668.5 17.2 %all-gather.4 = f32[8,1,256]{2,1,0:T(1,128)S(1)} all-gather(f32[1,1,256]{2,1,0:T(1,128)S(1)} %bitcast.142), channel_id=2, replica_groups=mesh['shot'=16,'tile'=8] {'tile'}, dimensions={0}, use_global_device_ids=true | all-gather | bytes 9216 | tf_op jit(solution)/shard_map/while/body/eval_jaxpr/all_gather | solution.py:165
  (384 shorter events, 275.0 us)
Async XLA Ops:
  7.2 52.4 %all-gather.9.cloned.1.call-start = ((), (), s32[]{:S(2)}) async-start(), calls=%async_computation.1 | async-start | bytes 2228224 | tf_op jit(solution)/shard_map/all_gather | solution.py:140
  7.9 100.6 %all-gather.13.cloned.1.call-start = ((), (), s32[]{:S(2)}) async-start(), calls=%async_computation.3 | async-start | bytes 2228224 | tf_op jit(solution)/shard_map/all_gather | solution.py:139
  8.6 148.8 %all-gather.11.cloned.1.call-start = ((), (), s32[]{:S(2)}) async-start(), calls=%async_computation.2 | async-start | bytes 2228224 | tf_op jit(solution)/shard_map/all_gather | solution.py:138
  9.4 678.6 %reduce-scatter.2.cloned.1.call-start = ((), (), s32[]{:S(2)}) async-start(), calls=%async_computation.4 | async-start | bytes 2228224 | tf_op jit(solution)/shard_map/reduce_scatter | solution.py:173
  180.6 25.1 %collective-permute-start.2 = (f32[3,4,32,256]{3,2,1,0:T(8,128)S(1)}, f32[3,4,32,256]{3,2,1,0:T(8,128)S(1)}, u32[]{:S(2)}, u32[]{:S(2)}) collective-permute-start(f32[3,4,32,256]{3,2,1,0:T(8,128)S(1)} %pad_maximum_fusion.10), channel_id=1, source_target_pairs={{1,0},{2,1},{3,2},{4,3},{5,4},{6,5},{7,6},{9,8},{10,9},{11,10},{12... | collective-permute-start | bytes 1179656 | tf_op jit(solution)/shard_map/while/body/eval_jaxpr/ppermute | solution.py:20
  182.5 23.1 %collective-permute-start.3 = (f32[3,4,32,256]{3,2,1,0:T(8,128)S(1)}, f32[3,4,32,256]{3,2,1,0:T(8,128)S(1)}, u32[]{:S(2)}, u32[]{:S(2)}) collective-permute-start(f32[3,4,32,256]{3,2,1,0:T(8,128)S(1)} %pad_maximum_fusion.10), channel_id=1, source_target_pairs={{0,1},{1,2},{2,3},{3,4},{4,5},{5,6},{6,7},{8,9},{9,10},{10,11},{11... | collective-permute-start | bytes 1179656 | tf_op jit(solution)/shard_map/while/body/eval_jaxpr/ppermute | solution.py:18
  225.9 25.0 %collective-permute-start.2 = (f32[3,4,32,256]{3,2,1,0:T(8,128)S(1)}, f32[3,4,32,256]{3,2,1,0:T(8,128)S(1)}, u32[]{:S(2)}, u32[]{:S(2)}) collective-permute-start(f32[3,4,32,256]{3,2,1,0:T(8,128)S(1)} %pad_maximum_fusion.10), channel_id=1, source_target_pairs={{1,0},{2,1},{3,2},{4,3},{5,4},{6,5},{7,6},{9,8},{10,9},{11,10},{12... | collective-permute-start | bytes 1179656 | tf_op jit(solution)/shard_map/while/body/eval_jaxpr/ppermute | solution.py:20
  227.8 23.1 %collective-permute-start.3 = (f32[3,4,32,256]{3,2,1,0:T(8,128)S(1)}, f32[3,4,32,256]{3,2,1,0:T(8,128)S(1)}, u32[]{:S(2)}, u32[]{:S(2)}) collective-permute-start(f32[3,4,32,256]{3,2,1,0:T(8,128)S(1)} %pad_maximum_fusion.10), channel_id=1, source_target_pairs={{0,1},{1,2},{2,3},{3,4},{4,5},{5,6},{6,7},{8,9},{9,10},{10,11},{11... | collective-permute-start | bytes 1179656 | tf_op jit(solution)/shard_map/while/body/eval_jaxpr/ppermute | solution.py:18
  269.0 25.0 %collective-permute-start.2 = (f32[3,4,32,256]{3,2,1,0:T(8,128)S(1)}, f32[3,4,32,256]{3,2,1,0:T(8,128)S(1)}, u32[]{:S(2)}, u32[]{:S(2)}) collective-permute-start(f32[3,4,32,256]{3,2,1,0:T(8,128)S(1)} %pad_maximum_fusion.10), channel_id=1, source_target_pairs={{1,0},{2,1},{3,2},{4,3},{5,4},{6,5},{7,6},{9,8},{10,9},{11,10},{12... | collective-permute-start | bytes 1179656 | tf_op jit(solution)/shard_map/while/body/eval_jaxpr/ppermute | solution.py:20
  270.9 23.1 %collective-permute-start.3 = (f32[3,4,32,256]{3,2,1,0:T(8,128)S(1)}, f32[3,4,32,256]{3,2,1,0:T(8,128)S(1)}, u32[]{:S(2)}, u32[]{:S(2)}) collective-permute-start(f32[3,4,32,256]{3,2,1,0:T(8,128)S(1)} %pad_maximum_fusion.10), channel_id=1, source_target_pairs={{0,1},{1,2},{2,3},{3,4},{4,5},{5,6},{6,7},{8,9},{9,10},{10,11},{11... | collective-permute-start | bytes 1179656 | tf_op jit(solution)/shard_map/while/body/eval_jaxpr/ppermute | solution.py:18
  312.9 25.0 %collective-permute-start.2 = (f32[3,4,32,256]{3,2,1,0:T(8,128)S(1)}, f32[3,4,32,256]{3,2,1,0:T(8,128)S(1)}, u32[]{:S(2)}, u32[]{:S(2)}) collective-permute-start(f32[3,4,32,256]{3,2,1,0:T(8,128)S(1)} %pad_maximum_fusion.10), channel_id=1, source_target_pairs={{1,0},{2,1},{3,2},{4,3},{5,4},{6,5},{7,6},{9,8},{10,9},{11,10},{12... | collective-permute-start | bytes 1179656 | tf_op jit(solution)/shard_map/while/body/eval_jaxpr/ppermute | solution.py:20
  314.8 23.1 %collective-permute-start.3 = (f32[3,4,32,256]{3,2,1,0:T(8,128)S(1)}, f32[3,4,32,256]{3,2,1,0:T(8,128)S(1)}, u32[]{:S(2)}, u32[]{:S(2)}) collective-permute-start(f32[3,4,32,256]{3,2,1,0:T(8,128)S(1)} %pad_maximum_fusion.10), channel_id=1, source_target_pairs={{0,1},{1,2},{2,3},{3,4},{4,5},{5,6},{6,7},{8,9},{9,10},{10,11},{11... | collective-permute-start | bytes 1179656 | tf_op jit(solution)/shard_map/while/body/eval_jaxpr/ppermute | solution.py:18
  354.7 26.5 %collective-permute-start.2 = (f32[3,4,32,256]{3,2,1,0:T(8,128)S(1)}, f32[3,4,32,256]{3,2,1,0:T(8,128)S(1)}, u32[]{:S(2)}, u32[]{:S(2)}) collective-permute-start(f32[3,4,32,256]{3,2,1,0:T(8,128)S(1)} %pad_maximum_fusion.10), channel_id=1, source_target_pairs={{1,0},{2,1},{3,2},{4,3},{5,4},{6,5},{7,6},{9,8},{10,9},{11,10},{12... | collective-permute-start | bytes 1179656 | tf_op jit(solution)/shard_map/while/body/eval_jaxpr/ppermute | solution.py:20
  356.6 24.6 %collective-permute-start.3 = (f32[3,4,32,256]{3,2,1,0:T(8,128)S(1)}, f32[3,4,32,256]{3,2,1,0:T(8,128)S(1)}, u32[]{:S(2)}, u32[]{:S(2)}) collective-permute-start(f32[3,4,32,256]{3,2,1,0:T(8,128)S(1)} %pad_maximum_fusion.10), channel_id=1, source_target_pairs={{0,1},{1,2},{2,3},{3,4},{4,5},{5,6},{6,7},{8,9},{9,10},{10,11},{11... | collective-permute-start | bytes 1179656 | tf_op jit(solution)/shard_map/while/body/eval_jaxpr/ppermute | solution.py:18
  400.3 25.0 %collective-permute-start.2 = (f32[3,4,32,256]{3,2,1,0:T(8,128)S(1)}, f32[3,4,32,256]{3,2,1,0:T(8,128)S(1)}, u32[]{:S(2)}, u32[]{:S(2)}) collective-permute-start(f32[3,4,32,256]{3,2,1,0:T(8,128)S(1)} %pad_maximum_fusion.10), channel_id=1, source_target_pairs={{1,0},{2,1},{3,2},{4,3},{5,4},{6,5},{7,6},{9,8},{10,9},{11,10},{12... | collective-permute-start | bytes 1179656 | tf_op jit(solution)/shard_map/while/body/eval_jaxpr/ppermute | solution.py:20
  442.0 25.0 %collective-permute-start.2 = (f32[3,4,32,256]{3,2,1,0:T(8,128)S(1)}, f32[3,4,32,256]{3,2,1,0:T(8,128)S(1)}, u32[]{:S(2)}, u32[]{:S(2)}) collective-permute-start(f32[3,4,32,256]{3,2,1,0:T(8,128)S(1)} %pad_maximum_fusion.10), channel_id=1, source_target_pairs={{1,0},{2,1},{3,2},{4,3},{5,4},{6,5},{7,6},{9,8},{10,9},{11,10},{12... | collective-permute-start | bytes 1179656 | tf_op jit(solution)/shard_map/while/body/eval_jaxpr/ppermute | solution.py:20
  444.0 23.1 %collective-permute-start.3 = (f32[3,4,32,256]{3,2,1,0:T(8,128)S(1)}, f32[3,4,32,256]{3,2,1,0:T(8,128)S(1)}, u32[]{:S(2)}, u32[]{:S(2)}) collective-permute-start(f32[3,4,32,256]{3,2,1,0:T(8,128)S(1)} %pad_maximum_fusion.10), channel_id=1, source_target_pairs={{0,1},{1,2},{2,3},{3,4},{4,5},{5,6},{6,7},{8,9},{9,10},{10,11},{11... | collective-permute-start | bytes 1179656 | tf_op jit(solution)/shard_map/while/body/eval_jaxpr/ppermute | solution.py:18
  486.6 26.7 %collective-permute-start.2 = (f32[3,4,32,256]{3,2,1,0:T(8,128)S(1)}, f32[3,4,32,256]{3,2,1,0:T(8,128)S(1)}, u32[]{:S(2)}, u32[]{:S(2)}) collective-permute-start(f32[3,4,32,256]{3,2,1,0:T(8,128)S(1)} %pad_maximum_fusion.10), channel_id=1, source_target_pairs={{1,0},{2,1},{3,2},{4,3},{5,4},{6,5},{7,6},{9,8},{10,9},{11,10},{12... | collective-permute-start | bytes 1179656 | tf_op jit(solution)/shard_map/while/body/eval_jaxpr/ppermute | solution.py:20
  488.6 24.8 %collective-permute-start.3 = (f32[3,4,32,256]{3,2,1,0:T(8,128)S(1)}, f32[3,4,32,256]{3,2,1,0:T(8,128)S(1)}, u32[]{:S(2)}, u32[]{:S(2)}) collective-permute-start(f32[3,4,32,256]{3,2,1,0:T(8,128)S(1)} %pad_maximum_fusion.10), channel_id=1, source_target_pairs={{0,1},{1,2},{2,3},{3,4},{4,5},{5,6},{6,7},{8,9},{9,10},{10,11},{11... | collective-permute-start | bytes 1179656 | tf_op jit(solution)/shard_map/while/body/eval_jaxpr/ppermute | solution.py:18
  532.5 25.0 %collective-permute-start.2 = (f32[3,4,32,256]{3,2,1,0:T(8,128)S(1)}, f32[3,4,32,256]{3,2,1,0:T(8,128)S(1)}, u32[]{:S(2)}, u32[]{:S(2)}) collective-permute-start(f32[3,4,32,256]{3,2,1,0:T(8,128)S(1)} %pad_maximum_fusion.10), channel_id=1, source_target_pairs={{1,0},{2,1},{3,2},{4,3},{5,4},{6,5},{7,6},{9,8},{10,9},{11,10},{12... | collective-permute-start | bytes 1179656 | tf_op jit(solution)/shard_map/while/body/eval_jaxpr/ppermute | solution.py:20
  574.2 25.0 %collective-permute-start.2 = (f32[3,4,32,256]{3,2,1,0:T(8,128)S(1)}, f32[3,4,32,256]{3,2,1,0:T(8,128)S(1)}, u32[]{:S(2)}, u32[]{:S(2)}) collective-permute-start(f32[3,4,32,256]{3,2,1,0:T(8,128)S(1)} %pad_maximum_fusion.10), channel_id=1, source_target_pairs={{1,0},{2,1},{3,2},{4,3},{5,4},{6,5},{7,6},{9,8},{10,9},{11,10},{12... | collective-permute-start | bytes 1179656 | tf_op jit(solution)/shard_map/while/body/eval_jaxpr/ppermute | solution.py:20
  576.2 23.1 %collective-permute-start.3 = (f32[3,4,32,256]{3,2,1,0:T(8,128)S(1)}, f32[3,4,32,256]{3,2,1,0:T(8,128)S(1)}, u32[]{:S(2)}, u32[]{:S(2)}) collective-permute-start(f32[3,4,32,256]{3,2,1,0:T(8,128)S(1)} %pad_maximum_fusion.10), channel_id=1, source_target_pairs={{0,1},{1,2},{2,3},{3,4},{4,5},{5,6},{6,7},{8,9},{9,10},{10,11},{11... | collective-permute-start | bytes 1179656 | tf_op jit(solution)/shard_map/while/body/eval_jaxpr/ppermute | solution.py:18
  619.0 25.0 %collective-permute-start.2 = (f32[3,4,32,256]{3,2,1,0:T(8,128)S(1)}, f32[3,4,32,256]{3,2,1,0:T(8,128)S(1)}, u32[]{:S(2)}, u32[]{:S(2)}) collective-permute-start(f32[3,4,32,256]{3,2,1,0:T(8,128)S(1)} %pad_maximum_fusion.10), channel_id=1, source_target_pairs={{1,0},{2,1},{3,2},{4,3},{5,4},{6,5},{7,6},{9,8},{10,9},{11,10},{12... | collective-permute-start | bytes 1179656 | tf_op jit(solution)/shard_map/while/body/eval_jaxpr/ppermute | solution.py:20
  660.8 25.0 %collective-permute-start.2 = (f32[3,4,32,256]{3,2,1,0:T(8,128)S(1)}, f32[3,4,32,256]{3,2,1,0:T(8,128)S(1)}, u32[]{:S(2)}, u32[]{:S(2)}) collective-permute-start(f32[3,4,32,256]{3,2,1,0:T(8,128)S(1)} %pad_maximum_fusion.10), channel_id=1, source_target_pairs={{1,0},{2,1},{3,2},{4,3},{5,4},{6,5},{7,6},{9,8},{10,9},{11,10},{12... | collective-permute-start | bytes 1179656 | tf_op jit(solution)/shard_map/while/body/eval_jaxpr/ppermute | solution.py:20
  (34 other events, 527.1 us)
Sparse Core Ops, SparseCore 0:
  10.4 49.0 all-gather.8
  62.0 46.4 all-gather.12
  111.0 46.4 all-gather.10
  161.7 70.1 reduce-scatter.1
